TPU v7x, 256 devices: a whole 4x4x8 slice. The times are simulated.
256 devices in a mesh: shard: 16 (over x, z_hi, core), rep: 16 (over y, z_lo).
Axes of the slice: x: 4, y: 4, z: 8 (z_hi: 2, z_lo: 4; z = z_hi * 4 + z_lo), core: 2. Of those that a mesh axis runs over, the one named last changes fastest.
Arguments:
- grads: bfloat16 [16, 16, 2097152], P('shard', 'rep'), may hold values from -5000 to 5000
- momentum_codes: int32 [2097152], P(('shard', 'rep')), may hold values from -127 to 127
- variance_codes: int32 [2097152], P(('shard', 'rep')), may hold values from 16 to 255
- momentum_scale: float32 [1280], P(('shard', 'rep')), may hold values from 0.5 to 4, as said below
- variance_scale: float32 [1280], P(('shard', 'rep')), may hold values from 1 to 4, as said below
- master: float32 [2097152], P(('shard', 'rep')), may hold values from -2.5 to 2.5
- step: int32 [1], replicated, may hold values from 1 to 19
Outputs:
- new_master: float32 [2097152], P(('shard', 'rep'))
- weights: bfloat16 [2097152], P('shard')
- update: float32 [2097152], P(('shard', 'rep'))
- momentum_norm: float32 [2097152], P(('shard', 'rep'))
- variance_norm: float32 [2097152], P(('shard', 'rep'))
- momentum_absmax: float32 [1280], P(('shard', 'rep'))
- variance_absmax: float32 [1280], P(('shard', 'rep'))
Inputs may be any that keep to these rules, and one draw needn't show every extreme that they name: `momentum_scale`: A block touched by two neighbouring devices has the same value in both devices' slots. `variance_scale`: A block touched by two neighbouring devices has the same value in both devices' slots.
All inputs are finite; a program needn't handle non-finite values.
Results may differ from a plain program's by a relative error of at most 0.0004.
Values may be sent and summed in bfloat16 or wider, within the bound.
A program may use at most 64 MiB of HBM per device.

v0:
```python
import jax
import jax.numpy as jnp
from jax import lax
from jax.sharding import PartitionSpec as P

BLOCK = 2048


def extended(block, sides, width):
    for axis, dim in sides:
        count = lax.axis_size(axis)
        forward = [(i, i + 1) for i in range(count - 1)]
        backward = [(target, source) for source, target in forward]
        low = lax.ppermute(
            lax.slice_in_dim(block, block.shape[dim] - width, None, axis=dim), axis, forward
        )
        high = lax.ppermute(lax.slice_in_dim(block, 0, width, axis=dim), axis, backward)
        block = jnp.concatenate([low, block, high], axis=dim)
    return block


def on_device(grads, momentum_codes, variance_codes, momentum_scale, variance_scale, master, step):
    own_len = master.shape[0]
    slot_count = momentum_scale.shape[0]
    block_len = BLOCK
    half_len = block_len // 2
    shard_count = lax.axis_size("shard")
    rep_count = lax.axis_size("rep")
    grad_terms = grads.reshape(-1).astype(jnp.float32)
    partial_sum = lax.psum_scatter(grad_terms, "shard", scatter_dimension=0, tiled=True)
    gsum = lax.psum_scatter(partial_sum, "rep", scatter_dimension=0, tiled=True)
    norm_sq = lax.psum(jnp.sum(gsum * gsum), ("shard", "rep"))
    total_params = own_len * shard_count * rep_count
    clip_factor = jnp.minimum(1.0, float(total_params) ** 0.5 / (jnp.sqrt(norm_sq) + 1e-06))
    scaled = gsum * clip_factor

    def spread(scale_table):
        return jnp.repeat(scale_table, block_len)[half_len : half_len + own_len]

    m_old = momentum_codes.astype(jnp.float32) / 127.0 * spread(momentum_scale)
    v_old = variance_codes.astype(jnp.float32) / 255.0 * spread(variance_scale)
    momentum = 0.9 * m_old + 0.1 * scaled
    variance = 0.95 * v_old + 0.05 * scaled * scaled
    count = step[0].astype(jnp.float32)
    first_fix = 1.0 - jnp.power(jnp.float32(0.9), count)
    second_fix = 1.0 - jnp.power(jnp.float32(0.95), count)
    update = momentum / first_fix / (jnp.sqrt(variance / second_fix) + 1e-08)
    new_master = master * (1.0 - 0.0001 * 0.1) - 0.0001 * update
    weights = lax.all_gather(new_master.astype(jnp.bfloat16), "rep", axis=0, tiled=True)

    def slot_max(values):
        padded = jnp.pad(jnp.abs(values), (half_len, half_len))
        return jnp.max(padded.reshape(slot_count, block_len), axis=1)

    m_table = slot_max(momentum)
    v_table = slot_max(variance)
    own_edge = jnp.stack(
        [jnp.stack([m_table[0], v_table[0]]), jnp.stack([m_table[-1], v_table[-1]])]
    )
    rim_vals = extended(own_edge, ((("shard", "rep"), 0),), 1)
    m_table = m_table.at[0].max(rim_vals[0, 0]).at[-1].max(rim_vals[3, 0])
    v_table = v_table.at[0].max(rim_vals[0, 1]).at[-1].max(rim_vals[3, 1])
    momentum_norm = momentum / (spread(m_table) + 1e-06)
    variance_norm = variance / (spread(v_table) + 1e-06)
    return (new_master, weights, update, momentum_norm, variance_norm, m_table, v_table)


def solution(mesh):
    in_specs = (
        P("shard", "rep", None),
        P(("shard", "rep")),
        P(("shard", "rep")),
        P(("shard", "rep")),
        P(("shard", "rep")),
        P(("shard", "rep")),
        P(),
    )
    out_specs = (
        P(("shard", "rep")),
        P("shard"),
        P(("shard", "rep")),
        P(("shard", "rep")),
        P(("shard", "rep")),
        P(("shard", "rep")),
        P(("shard", "rep")),
    )
    return jax.shard_map(
        on_device, mesh=mesh, in_specs=in_specs, out_specs=out_specs, check_vma=False
    )
```

profile of v0, /device:TPU:2, one launch (start us, length us, event | category | flops | bytes accessed | tf_op | source)
XLA Modules:
  0.0 717.0 jit_solution(4956482309576053359)
XLA Ops:
  7.2 10.8 %convert_element_type.28 = f32[1,1,2097152]{2,1,0:T(1,128)} convert(bf16[1,1,2097152]{2,1,0:T(2,128)(2,1)} %param.15) | non-fusion elementwise | flops 2097152 | bytes 12582912 | tf_op jit(solution)/shard_map/convert_element_type | solution.py:29
  20.0 379.7 %all-reduce.7.cloned.1.call-done = f32[2097152]{0:T(1024)} async-done(((f32[2097152]{0:T(1024)}), f32[2097152]{0:T(1024)}) %all-reduce.7.cloned.1.call-update) | async-done | bytes 8388624
  399.7 1.9 dynamic-slice.25
  401.7 0.6 dynamic-slice.26
  403.8 161.5 %all-reduce.9.cloned.1.call-done = f32[131072]{0:T(1024)} async-done(((f32[131072]{0:T(1024)}), f32[131072]{0:T(1024)}) %all-reduce.9.cloned.1.call-update) | async-done | bytes 524304
  565.3 1.4 multiply_reduce_fusion
  566.7 75.3 %psum.7 = f32[]{:T(128)} all-reduce(f32[]{:T(128)} %multiply_reduce_fusion), channel_id=1, replica_groups=mesh['shard'=16,'rep'=16] {'shard','rep'}, use_global_device_ids=true, to_apply=%region_3.0 | all-reduce | flops 1 | bytes 8 | tf_op jit(solution)/shard_map/psum | solution.py:32
  642.7 0.8 fusion.6
  643.7 0.6 slice.84
  644.4 0.6 slice.83
  645.0 1.4 maximum_bitcast_fusion
  646.4 1.9 collective-permute-start
  648.3 7.2 %collective-permute-done = f32[1,2]{1,0:T(1,128)S(1)} collective-permute-done((f32[1,2]{1,0:T(1,128)S(1)}, f32[1,2]{1,0:T(1,128)S(1)}, u32[]{:S(2)}, u32[]{:S(2)}) %collective-permute-start) | collective-permute-done | bytes 40 | tf_op jit(solution)/shard_map/ppermute | solution.py:14
  655.5 0.6 fusion.12
  656.0 1.8 constant_dynamic-update-slice_fusion.2
  657.9 1.4 maximum_bitcast_fusion.1
  659.2 1.9 collective-permute-start.1
  661.1 3.5 collective-permute-done.1
  664.7 0.6 fusion.11
  665.3 0.8 constant_dynamic-update-slice_fusion
  666.1 0.8 constant_dynamic-update-slice_fusion.1
  667.1 0.7 fusion.10
  667.7 41.7 %all_gather.3 = bf16[131072]{0:T(1024)(128)(2,1)S(1)} all-gather(bf16[8192]{0:T(1024)(128)(2,1)S(1)} %get-tuple-element.59), channel_id=1, replica_groups=mesh['shard'=16,'rep'=16] {'rep'}, dimensions={0}, use_global_device_ids=true | all-gather | bytes 278528 | tf_op jit(solution)/shard_map/all_gather | solution.py:49
  709.5 0.7 copy.22
  (37 shorter events, 1.9 us)
Async XLA Ops:
  7.2 392.5 %all-reduce.7.cloned.1.call-start = ((), (), s32[]{:S(2)}) async-start(), calls=%async_computation | async-start | bytes 16777216
  18.1 0.7 copy-start.8
  18.1 383.6 %copy-start.7 = (u32[256]{0:T(256)S(1)}, u32[256]{0:T(256)}, u32[]{:S(2)}) copy-start(u32[256]{0:T(256)} %constant.134) | copy-start | bytes 3076
  18.1 384.2 %copy-start.5 = (f32[5]{0:T(128)S(1)}, f32[5]{0:T(128)}, u32[]{:S(2)}) copy-start(f32[5]{0:T(128)} %param.19) | copy-start | bytes 64
  18.1 384.3 %copy-start.6 = (f32[5]{0:T(128)S(1)}, f32[5]{0:T(128)}, u32[]{:S(2)}) copy-start(f32[5]{0:T(128)} %param.18) | copy-start | bytes 64
  18.1 624.6 %copy-start = (s32[8192]{0:T(1024)S(1)}, s32[8192]{0:T(1024)}, u32[]{:S(2)}) copy-start(s32[8192]{0:T(1024)} %param.17) | copy-start | bytes 98308
  18.1 624.6 %copy-start.1 = (s32[8192]{0:T(1024)S(1)}, s32[8192]{0:T(1024)}, u32[]{:S(2)}) copy-start(s32[8192]{0:T(1024)} %param.16) | copy-start | bytes 98308
  18.1 648.9 %copy-start.2 = (f32[8192]{0:T(1024)S(1)}, f32[8192]{0:T(1024)}, u32[]{:S(2)}) copy-start(f32[8192]{0:T(1024)} %param.20) | copy-start | bytes 98308
  18.2 547.1 %all-reduce.9.cloned.1.call-start = ((), (), s32[]{:S(2)}) async-start(), calls=%async_computation.1 | async-start | bytes 1048576
  646.4 9.1 %collective-permute-start = (f32[1,2]{1,0:T(1,128)S(1)}, f32[1,2]{1,0:T(1,128)S(1)}, u32[]{:S(2)}, u32[]{:S(2)}) collective-permute-start(f32[1,2]{1,0:T(1,128)S(1)} %maximum_bitcast_fusion), channel_id=1, source_target_pairs={{0,1},{1,2},{2,3},{3,4},{4,5},{5,6},{6,7},{7,8},{8,9},{9,10},{10,1... | collective-permute-start | bytes 32 | tf_op jit(solution)/shard_map/ppermute | solution.py:14
  659.2 5.5 collective-permute-start.1
  666.1 44.2 %copy-start.3 = (f32[5]{0:T(128)}, f32[5]{0:T(128)S(1)}, u32[]{:S(2)}) copy-start(f32[5]{0:T(128)S(1)} %constant_dynamic-update-slice_fusion) | copy-start | bytes 64
  666.9 43.3 %copy-start.4 = (f32[5]{0:T(128)}, f32[5]{0:T(128)S(1)}, u32[]{:S(2)}) copy-start(f32[5]{0:T(128)S(1)} %constant_dynamic-update-slice_fusion.1) | copy-start | bytes 64
Sparse Core Ops, SparseCore 0:
  18.3 381.3 all-reduce.6
  402.3 162.9 all-reduce.8
where the time goes:
time: 718 us; the launch traced here: 717 us
  waiting for transfers between devices  552 us (77%)
  blocking collectives  117 us (16%)
  other arithmetic  20.1 us (3%)
  between operations  17 us (2%)
    unnamed x4, waiting for transfers between devices  541 us
    psum x1, blocking collectives, on_device(): norm_sq = lax.psum(jnp.sum(gsum * gsum), ('shard', 'rep'))  75.3 us
    all_gather x1, blocking collectives, on_device(): lax.all_gather(new_master.astype(jnp.bfloat16), 'rep', axis=0, tiled=True)  41.7 us
  transfers between devices with their start and end apart: 4, of which 4 were waited for; matrix products, arithmetic and copies ran while one was open for 0% of the time, Pallas kernels for 0%

commit v1 on v0

--- a/solution.py
+++ b/solution.py
@@ -46,7 +46,12 @@
     second_fix = 1.0 - jnp.power(jnp.float32(0.95), count)
     update = momentum / first_fix / (jnp.sqrt(variance / second_fix) + 1e-08)
     new_master = master * (1.0 - 0.0001 * 0.1) - 0.0001 * update
-    weights = lax.all_gather(new_master.astype(jnp.bfloat16), "rep", axis=0, tiled=True)
+    weights = jnp.concatenate(
+        lax.all_to_all(
+            jnp.stack([new_master.astype(jnp.bfloat16)] * lax.axis_size("rep")), "rep", 0, 0
+        ),
+        axis=0,
+    )
 
     def slot_max(values):
         padded = jnp.pad(jnp.abs(values), (half_len, half_len))

time: 718 us -> 696 us (0.969)
  blocking collectives: 117 us -> 90 us
    all_gather x1 -> x0, blocking collectives: 41.7 us -> none  [on_device(): lax.all_gather(new_master.astype(jnp.bfloat16), 'rep', axis=0, tiled=True)]
    all_to_all x0 -> x1, blocking collectives: none -> 14.6 us  [on_device(): lax.all_to_all(jnp.stack([new_master.astype(jnp.bfloat16)] * lax.axis_siz...]
where the time goes in v1:
time: 696 us; the launch traced here: 695 us
  waiting for transfers between devices  552 us (79%)
  blocking collectives  90 us (13%)
  other arithmetic  23.8 us (3%)
  between operations  17 us (2%)
  local copies, waits for them, and re-layouts  8.5 us (1%)
    unnamed x4, waiting for transfers between devices  541 us
    psum x1, blocking collectives, on_device(): norm_sq = lax.psum(jnp.sum(gsum * gsum), ('shard', 'rep'))  75.3 us
    all_to_all x1, blocking collectives, on_device(): lax.all_to_all(jnp.stack([new_master.astype(jnp.bfloat16)] * lax.axis_siz...  14.6 us
  transfers between devices with their start and end apart: 4, of which 4 were waited for; matrix products, arithmetic and copies ran while one was open for 0% of the time, Pallas kernels for 0%

profile of v1, /device:TPU:2, one launch (start us, length us, event | category | flops | bytes accessed | tf_op | source)
XLA Modules:
  0.0 695.1 jit_solution(493162126669365185)
XLA Ops:
  7.2 10.8 %convert_element_type.28 = f32[1,1,2097152]{2,1,0:T(1,128)} convert(bf16[1,1,2097152]{2,1,0:T(2,128)(2,1)} %param.15) | non-fusion elementwise | flops 2097152 | bytes 12582912 | tf_op jit(solution)/shard_map/convert_element_type | solution.py:29
  20.0 379.7 %all-reduce.7.cloned.1.call-done = f32[2097152]{0:T(1024)} async-done(((f32[2097152]{0:T(1024)}), f32[2097152]{0:T(1024)}) %all-reduce.7.cloned.1.call-update) | async-done | bytes 8388624
  399.7 1.9 dynamic-slice.25
  401.6 0.6 dynamic-slice.26
  403.8 161.5 %all-reduce.9.cloned.1.call-done = f32[131072]{0:T(1024)} async-done(((f32[131072]{0:T(1024)}), f32[131072]{0:T(1024)}) %all-reduce.9.cloned.1.call-update) | async-done | bytes 524304
  565.3 1.4 multiply_reduce_fusion
  566.6 75.3 %psum.7 = f32[]{:T(128)} all-reduce(f32[]{:T(128)} %multiply_reduce_fusion), channel_id=1, replica_groups=mesh['shard'=16,'rep'=16] {'shard','rep'}, use_global_device_ids=true, to_apply=%region_3.0 | all-reduce | flops 1 | bytes 8 | tf_op jit(solution)/shard_map/psum | solution.py:32
  642.7 0.8 fusion.6
  643.7 0.6 slice.84
  644.4 0.6 slice.83
  645.0 1.4 maximum_bitcast_fusion
  646.4 1.9 collective-permute-start
  648.3 7.2 %collective-permute-done = f32[1,2]{1,0:T(1,128)S(1)} collective-permute-done((f32[1,2]{1,0:T(1,128)S(1)}, f32[1,2]{1,0:T(1,128)S(1)}, u32[]{:S(2)}, u32[]{:S(2)}) %collective-permute-start) | collective-permute-done | bytes 40 | tf_op jit(solution)/shard_map/ppermute | solution.py:14
  656.0 1.8 constant_dynamic-update-slice_fusion.2
  657.8 1.4 maximum_bitcast_fusion.1
  659.2 1.9 collective-permute-start.1
  661.1 3.5 collective-permute-done.1
  665.2 0.8 constant_dynamic-update-slice_fusion
  666.1 0.8 constant_dynamic-update-slice_fusion.1
  667.0 0.7 fusion.10
  668.6 2.2 reduce.9
  671.0 14.6 %all_to_all.6 = bf16[16,2,4096]{2,1,0:T(2,128)(2,1)S(1)} all-to-all(bf16[16,2,4096]{2,1,0:T(2,128)(2,1)S(1)} %reshape.155), channel_id=1, replica_groups=mesh['shard'=16,'rep'=16] {'rep'}, dimensions={0} | all-to-all | bytes 524288 | tf_op jit(solution)/shard_map/all_to_all | solution.py:50
  685.9 1.5 reduce.8
  687.5 0.8 copy.14
  (43 shorter events, 4.5 us)
Async XLA Ops:
  7.2 392.5 %all-reduce.7.cloned.1.call-start = ((), (), s32[]{:S(2)}) async-start(), calls=%async_computation.1 | async-start | bytes 16777216
  18.0 0.7 copy-start.8
  18.0 383.6 %copy-start.7 = (u32[256]{0:T(256)S(1)}, u32[256]{0:T(256)}, u32[]{:S(2)}) copy-start(u32[256]{0:T(256)} %constant.134) | copy-start | bytes 3076
  18.1 384.2 %copy-start.5 = (f32[5]{0:T(128)S(1)}, f32[5]{0:T(128)}, u32[]{:S(2)}) copy-start(f32[5]{0:T(128)} %param.19) | copy-start | bytes 64
  18.1 384.3 %copy-start.6 = (f32[5]{0:T(128)S(1)}, f32[5]{0:T(128)}, u32[]{:S(2)}) copy-start(f32[5]{0:T(128)} %param.18) | copy-start | bytes 64
  18.1 624.6 %copy-start = (s32[8192]{0:T(1024)S(1)}, s32[8192]{0:T(1024)}, u32[]{:S(2)}) copy-start(s32[8192]{0:T(1024)} %param.17) | copy-start | bytes 98308
  18.1 624.6 %copy-start.1 = (s32[8192]{0:T(1024)S(1)}, s32[8192]{0:T(1024)}, u32[]{:S(2)}) copy-start(s32[8192]{0:T(1024)} %param.16) | copy-start | bytes 98308
  18.1 648.9 %copy-start.2 = (f32[8192]{0:T(1024)S(1)}, f32[8192]{0:T(1024)}, u32[]{:S(2)}) copy-start(f32[8192]{0:T(1024)} %param.20) | copy-start | bytes 98308
  18.1 547.1 %all-reduce.9.cloned.1.call-start = ((), (), s32[]{:S(2)}) async-start(), calls=%async_computation.2 | async-start | bytes 1048576
  646.4 9.1 %collective-permute-start = (f32[1,2]{1,0:T(1,128)S(1)}, f32[1,2]{1,0:T(1,128)S(1)}, u32[]{:S(2)}, u32[]{:S(2)}) collective-permute-start(f32[1,2]{1,0:T(1,128)S(1)} %maximum_bitcast_fusion), channel_id=1, source_target_pairs={{0,1},{1,2},{2,3},{3,4},{4,5},{5,6},{6,7},{7,8},{8,9},{9,10},{10,1... | collective-permute-start | bytes 32 | tf_op jit(solution)/shard_map/ppermute | solution.py:14
  659.2 5.5 collective-permute-start.1
  666.0 22.2 %copy-start.3 = (f32[5]{0:T(128)}, f32[5]{0:T(128)S(1)}, u32[]{:S(2)}) copy-start(f32[5]{0:T(128)S(1)} %constant_dynamic-update-slice_fusion) | copy-start | bytes 64
  666.9 21.3 %copy-start.4 = (f32[5]{0:T(128)}, f32[5]{0:T(128)S(1)}, u32[]{:S(2)}) copy-start(f32[5]{0:T(128)S(1)} %constant_dynamic-update-slice_fusion.1) | copy-start | bytes 64
Sparse Core Ops, SparseCore 0:
  18.3 381.3 all-reduce.6
  402.3 162.9 all-reduce.8
